TPU v7x, 512 devices: a whole 4x4x16 slice. The times are simulated.
512 devices in a mesh: pairs: 128 (over x, z, core), rep: 4 (over y).
Axes of the slice: x: 4, y: 4, z: 16, core: 2. Of those that a mesh axis runs over, the one named last changes fastest.
Arguments:
- positions: float32 [3, 2048, 256], P(None, 'pairs'), may hold values from -1 to 1
- facing: float32 [2, 2048, 256], P(None, 'pairs'), may hold values from -3.140625 to 3.140625
- area: float32 [2048, 256], P('pairs'), may hold values from 0.00390625 to 0.03125
- emission: float32 [2048, 8, 256], P('pairs'), may hold values from 0.1 to 2
- reflect: float32 [2048, 8, 256], P('pairs'), may hold values from 0.2 to 0.9
- pair_list: int32 [128, 4, 128, 1, 2], P('pairs', 'rep'), may hold values from -1 to 2047, as said below
Outputs:
- radiosity: float32 [2048, 8, 256], P('pairs')
Inputs may be any that keep to these rules, and one draw needn't show every extreme that they name: `pair_list`: entry [p, r, q, c] is held by the device at pairs index p and rep index r in its slot c toward pairs index q. Its row block lies in p * 16 to (p + 1) * 16 - 1 and its column block in q * 16 to (q + 1) * 16 - 1, or both entries are -1 for an empty slot. Slots toward pairs index 0 are never empty.
All inputs are finite; a program needn't handle non-finite values.
Results may differ from a plain program's by a relative error of at most 0.0003.
Values may be sent and summed in bfloat16 or wider, within the bound.
A program may use at most 64 MiB of HBM per device.

v0:
```python
import jax
import jax.numpy as jnp
from jax import lax
from jax.sharding import PartitionSpec as P

SWEEPS = 2
soften = 0.1
group_tiles = 8


def unit_normals(facing):
    azimuth = facing[0]
    elevation = facing[1]
    return jnp.stack(
        [
            jnp.cos(azimuth) * jnp.cos(elevation),
            jnp.sin(azimuth) * jnp.cos(elevation),
            jnp.sin(elevation),
        ],
        axis=0,
    )


def pack_geometry(positions, facing):
    normals = unit_normals(facing)
    return jnp.transpose(jnp.concatenate([positions, normals], axis=0), (1, 0, 2))


def coupling(row_geom, col_geom):
    offsets = [
        col_geom[:, axis_id, None, :] - row_geom[:, axis_id, :, None] for axis_id in range(3)
    ]
    spread = offsets[0] * offsets[0] + offsets[1] * offsets[1] + offsets[2] * offsets[2] + soften
    nearside = (
        row_geom[:, 3, :, None] * offsets[0]
        + row_geom[:, 4, :, None] * offsets[1]
        + row_geom[:, 5, :, None] * offsets[2]
    )
    farside = (
        col_geom[:, 3, None, :] * offsets[0]
        + col_geom[:, 4, None, :] * offsets[1]
        + col_geom[:, 5, None, :] * offsets[2]
    )
    coupled = jnp.maximum(nearside, 0.0) * jnp.maximum(-farside, 0.0) / (jnp.pi * spread * spread)
    return coupled.astype(jnp.bfloat16)


def compact(active):
    slots = active.shape[0]
    flags = active.astype(jnp.int32)
    live_count = jnp.sum(flags)
    position = jnp.where(active, jnp.cumsum(flags) - 1, slots + group_tiles)
    ordering = jnp.full((slots + group_tiles,), slots, jnp.int32)
    ordering = ordering.at[position].set(jnp.arange(slots, dtype=jnp.int32), mode="drop")
    return (ordering, live_count)


def over_tiles(ordering, live_count, visit, initial):
    turns = (live_count + group_tiles - 1) // group_tiles

    def one_turn(turn_index, carry):
        slot_ids = lax.dynamic_slice_in_dim(ordering, turn_index * group_tiles, group_tiles)
        return visit(carry, slot_ids)

    return lax.fori_loop(0, turns, one_turn, initial)


def block_sum(block_ids, valid, terms, blocks):
    selector = (
        (block_ids[:, None] == jnp.arange(blocks, dtype=jnp.int32)[None, :]) & valid[:, None]
    ).astype(jnp.float32)
    return jnp.einsum("gk,gbi->kbi", selector, terms, precision=lax.Precision.HIGHEST)


def pair_kernel(slot_ids, row_local, geometry, col_geometry):
    slots = row_local.shape[0]
    valid = slot_ids < slots
    safe = jnp.minimum(slot_ids, slots - 1)
    row_ids = jnp.where(valid, jnp.take(row_local, safe), 0)
    kernel = coupling(jnp.take(geometry, row_ids, axis=0), jnp.take(col_geometry, safe, axis=0))
    return (valid, safe, row_ids, kernel)


def shards(positions, facing, area, emission, reflect, pair_list):
    blocks = area.shape[0]
    bands = emission.shape[1]
    patches = emission.shape[2]
    owners = lax.axis_size("pairs")
    geometry = pack_geometry(positions, facing)
    held = pair_list[0, 0]
    capacity = held.shape[1]
    slots = owners * capacity
    row_local = jnp.where(held[:, :, 0] >= 0, held[:, :, 0] % blocks, -1).reshape(slots)
    col_local = jnp.where(held[:, :, 1] >= 0, held[:, :, 1] % blocks, -1)
    requests = lax.all_to_all(col_local, "pairs", split_axis=0, concat_axis=0, tiled=True)
    served = jnp.take(geometry, jnp.clip(requests, 0, blocks - 1), axis=0)
    col_geometry = lax.all_to_all(served, "pairs", split_axis=0, concat_axis=0, tiled=True).reshape(
        slots, 6, patches
    )
    ordering, live_count = compact(row_local >= 0)
    wanted = requests.reshape(slots)
    owner_select = (wanted[:, None] == jnp.arange(blocks, dtype=jnp.int32)[None, :]).astype(
        jnp.float32
    )
    empty_sum = jnp.zeros((blocks, bands, patches), jnp.float32)
    radiosity = emission
    for sweep_index in range(SWEEPS):
        weighted = (area[:, None, :] * radiosity).astype(jnp.bfloat16)
        served_weights = jnp.take(weighted, jnp.clip(requests, 0, blocks - 1), axis=0)
        fetched = lax.all_to_all(served_weights, "pairs", split_axis=0, concat_axis=0, tiled=True)
        col_weights = fetched.reshape(slots, bands, patches)

        def both_visit(carry, slot_ids):
            row_part, returned = carry
            valid, safe, row_ids, kernel = pair_kernel(slot_ids, row_local, geometry, col_geometry)
            row_terms = jnp.einsum(
                "gij,gbj->gbi",
                kernel,
                jnp.take(col_weights, safe, axis=0),
                preferred_element_type=jnp.float32,
            )
            col_terms = jnp.einsum(
                "gij,gbi->gbj",
                kernel,
                jnp.take(weighted, row_ids, axis=0),
                preferred_element_type=jnp.float32,
            )
            row_part = row_part + block_sum(row_ids, valid, row_terms, blocks)
            returned = returned.at[jnp.where(valid, slot_ids, slots)].set(col_terms, mode="drop")
            return (row_part, returned)

        row_sum, returned = over_tiles(
            ordering,
            live_count,
            both_visit,
            (empty_sum, jnp.zeros((slots, bands, patches), jnp.float32)),
        )
        landed = lax.all_to_all(
            returned.reshape(owners, capacity, bands, patches),
            "pairs",
            split_axis=0,
            concat_axis=0,
            tiled=True,
        )
        incoming = jnp.einsum(
            "sk,sbp->kbp",
            owner_select,
            landed.reshape(slots, bands, patches),
            precision=lax.Precision.HIGHEST,
        )
        gathered = lax.psum(row_sum + incoming, "rep")
        radiosity = emission + reflect * gathered
    return radiosity


def solution(mesh):
    placed = (
        P(None, "pairs", None),
        P(None, "pairs", None),
        P("pairs", None),
        P("pairs", None, None),
        P("pairs", None, None),
        P("pairs", "rep", None, None, None),
    )
    return jax.shard_map(
        shards, mesh=mesh, in_specs=placed, out_specs=P("pairs", None, None), check_vma=False
    )
```

profile of v0, /device:TPU:2, one launch (start us, length us, event | category | flops | bytes accessed | tf_op | source)
XLA Modules:
  0.0 799.7 jit_solution(11148665395816167960)
XLA Ops:
  10.4 19.5 %all-to-all-start = ((s32[128,1,1]{2,1,0:T(1,128)}), s32[128,1,1]{2,1,0:T(1,128)S(1)}, u32[]{:S(2)}, u32[]{:S(2)}) async-start(s32[128,1,1]{2,1,0:T(1,128)} %get-tuple-element.351), calls=%async_computation | async-start | bytes 131072 | tf_op jit(solution)/shard_map/all_to_all | solution.py:95
  31.8 12.5 %all-to-all-done = s32[128,1,1]{2,1,0:T(1,128)S(1)} async-done(((s32[128,1,1]{2,1,0:T(1,128)}), s32[128,1,1]{2,1,0:T(1,128)S(1)}, u32[]{:S(2)}, u32[]{:S(2)}) %all-to-all-start) | async-done | bytes 544 | tf_op jit(solution)/shard_map/all_to_all | solution.py:95
  51.9 7.4 all-to-all-start.2
  59.4 4.6 fusion.83
  65.7 38.4 %all-to-all-done.2 = f32[128,1,6,256]{3,1,2,0:T(1,128)S(1)} async-done(((f32[128,1,6,256]{3,1,2,0:T(1,128)}), f32[128,1,6,256]{3,1,2,0:T(1,128)S(1)}, u32[]{:S(2)}, u32[]{:S(2)}) %all-to-all-start.2) | async-done | bytes 786464 | tf_op jit(solution)/shard_map/all_to_all | solution.py:97
  104.1 6.7 all-to-all-start.1
  113.7 30.7 %all-to-all-done.1 = bf16[128,1,8,256]{3,2,1,0:T(8,128)(2,1)S(1)} async-done(((bf16[128,1,8,256]{3,2,1,0:T(8,128)(2,1)}), bf16[128,1,8,256]{3,2,1,0:T(8,128)(2,1)S(1)}, u32[]{:S(2)}, u32[]{:S(2)}) %all-to-all-start.1) | async-done | bytes 524320 | tf_op jit(solution)/shard_map/all_to_all | solution.py:110
  144.5 57.7 %while.24 = (s32[]{:T(128)}, f32[16,8,256]{2,0,1:T(8,128)S(1)}, f32[128,8,256]{2,1,0:T(8,128)S(1)}, s32[]{:T(128)}, s32[136]{0:T(256)S(1)}, /*index=5*/s32[128]{...) while((s32[]{:T(128)}, f32[16,8,256]{2,0,1:T(8,128)S(1)}, ...), condition=%wide.region_5.12_spmd, body=%wide.region_3.11_spmd.sunk | while | flops 48327124 | bytes 1844099 | solution.py:65
  147.4 3.5 fusion.119
  152.2 3.5 fusion.118
  158.9 3.5 fusion.119
  163.7 3.5 fusion.118
  170.4 3.5 fusion.119
  175.3 3.5 fusion.118
  182.0 3.5 fusion.119
  186.8 3.5 fusion.118
  193.5 3.5 fusion.119
  198.3 3.5 fusion.118
  202.2 189.1 %all_to_all.31 = f32[128,1,8,256]{3,2,1,0:T(8,128)S(1)} all-to-all(f32[128,1,8,256]{3,2,1,0:T(8,128)S(1)} %bitcast.135), channel_id=1, replica_groups=mesh['pairs'=128,'rep'=4] {'pairs'}, dimensions={0} | all-to-all | bytes 2097152 | tf_op jit(solution)/shard_map/all_to_all | solution.py:138
  392.7 49.1 %all-reduce.3.cloned.1.call-done = f32[16,8,256]{2,0,1:T(8,128)} async-done(((f32[16,8,256]{2,0,1:T(8,128)}), f32[16,8,256]{2,0,1:T(8,128)}) %all-reduce.3.cloned.1.call-update) | async-done | bytes 131088 | tf_op jit(solution)/shard_map/psum | solution.py:151
  444.5 16.6 %all-to-all-start.4 = ((bf16[128,1,8,256]{3,2,1,0:T(8,128)(2,1)}), bf16[128,1,8,256]{3,2,1,0:T(8,128)(2,1)S(1)}, u32[]{:S(2)}, u32[]{:S(2)}) async-start(bf16[128,1,8,256]{3,2,1,0:T(8,128)(2,1)} %fusion.66), calls=%async_computation.4 | async-start | bytes 1048576 | tf_op jit(solution)/shard_map/all_to_all | solution.py:110
  461.2 33.5 %all-to-all-done.4 = bf16[128,1,8,256]{3,2,1,0:T(8,128)(2,1)S(1)} async-done(((bf16[128,1,8,256]{3,2,1,0:T(8,128)(2,1)}), bf16[128,1,8,256]{3,2,1,0:T(8,128)(2,1)S(1)}, u32[]{:S(2)}, u32[]{:S(2)}) %all-to-all-start.4) | async-done | bytes 524320 | tf_op jit(solution)/shard_map/all_to_all | solution.py:110
  494.8 57.7 %while.25 = (s32[]{:T(128)}, f32[16,8,256]{2,0,1:T(8,128)S(1)}, f32[128,8,256]{2,1,0:T(8,128)S(1)}, s32[]{:T(128)}, s32[136]{0:T(256)S(1)}, /*index=5*/s32[128]{...) while((s32[]{:T(128)}, f32[16,8,256]{2,0,1:T(8,128)S(1)}, ...), condition=%wide.region_9.16_spmd, body=%wide.region_7.15_spmd.sunk | while | flops 48327124 | bytes 1844099 | solution.py:65
  497.7 3.5 fusion.129
  509.2 3.5 fusion.129
  514.0 3.5 fusion.128
  520.8 3.5 fusion.129
  525.6 3.5 fusion.128
  532.3 3.5 fusion.129
  543.8 3.5 fusion.129
  552.5 189.1 %all_to_all.32 = f32[128,1,8,256]{3,2,1,0:T(8,128)S(1)} all-to-all(f32[128,1,8,256]{3,2,1,0:T(8,128)S(1)} %bitcast.134), channel_id=1, replica_groups=mesh['pairs'=128,'rep'=4] {'pairs'}, dimensions={0} | all-to-all | bytes 2097152 | tf_op jit(solution)/shard_map/all_to_all | solution.py:138
  743.0 48.1 %all-reduce.5.cloned.1.call-done = f32[16,8,256]{2,0,1:T(8,128)} async-done(((f32[16,8,256]{2,0,1:T(8,128)}), f32[16,8,256]{2,0,1:T(8,128)}) %all-reduce.5.cloned.1.call-update) | async-done | bytes 131088 | tf_op jit(solution)/shard_map/psum | solution.py:151
  (283 shorter events, 78.5 us)
Async XLA Ops:
  10.4 33.9 %all-to-all-start = ((s32[128,1,1]{2,1,0:T(1,128)}), s32[128,1,1]{2,1,0:T(1,128)S(1)}, u32[]{:S(2)}, u32[]{:S(2)}) async-start(s32[128,1,1]{2,1,0:T(1,128)} %get-tuple-element.351), calls=%async_computation | async-start | bytes 131072 | tf_op jit(solution)/shard_map/all_to_all | solution.py:95
  51.8 7.4 copy-start
  51.9 7.4 copy-start.2
  51.9 52.3 %all-to-all-start.2 = ((f32[128,1,6,256]{3,1,2,0:T(1,128)}), f32[128,1,6,256]{3,1,2,0:T(1,128)S(1)}, u32[]{:S(2)}, u32[]{:S(2)}) async-start(f32[128,1,6,256]{3,1,2,0:T(1,128)} %copy.141), calls=%async_computation.2 | async-start | bytes 1572864 | tf_op jit(solution)/shard_map/all_to_all | solution.py:97
  104.1 40.3 %all-to-all-start.1 = ((bf16[128,1,8,256]{3,2,1,0:T(8,128)(2,1)}), bf16[128,1,8,256]{3,2,1,0:T(8,128)(2,1)S(1)}, u32[]{:S(2)}, u32[]{:S(2)}) async-start(bf16[128,1,8,256]{3,2,1,0:T(8,128)(2,1)} %fusion.67), calls=%async_computation.1 | async-start | bytes 1048576 | tf_op jit(solution)/shard_map/all_to_all | solution.py:110
  110.8 331.1 %all-reduce.3.cloned.1.call-start = ((), (), s32[]{:S(2)}) async-start(), calls=%async_computation.6 | async-start | bytes 262144 | tf_op jit(solution)/shard_map/psum | solution.py:151
  391.3 50.6 %copy-start.1 = (f32[16,8,256]{2,1,0:T(8,128)S(1)}, f32[16,8,256]{2,1,0:T(8,128)}, u32[]{:S(2)}) copy-start(f32[16,8,256]{2,1,0:T(8,128)} %param.26) | copy-start | bytes 393220
  444.5 50.2 %all-to-all-start.4 = ((bf16[128,1,8,256]{3,2,1,0:T(8,128)(2,1)}), bf16[128,1,8,256]{3,2,1,0:T(8,128)(2,1)S(1)}, u32[]{:S(2)}, u32[]{:S(2)}) async-start(bf16[128,1,8,256]{3,2,1,0:T(8,128)(2,1)} %fusion.66), calls=%async_computation.4 | async-start | bytes 1048576 | tf_op jit(solution)/shard_map/all_to_all | solution.py:110
  461.2 329.9 %all-reduce.5.cloned.1.call-start = ((), (), s32[]{:S(2)}) async-start(), calls=%async_computation.7 | async-start | bytes 262144 | tf_op jit(solution)/shard_map/psum | solution.py:151
Sparse Core Ops, SparseCore 0:
  392.8 48.9 all-reduce.2
  743.1 47.9 all-reduce.4
where the time goes:
time: 800 us
  blocking collectives  378 us (47%)
  waiting for transfers between devices  212 us (26%)
  matrix products  76.4 us (10%)
  starting transfers between devices  50.3 us (6%)
  local copies, waits for them, and re-layouts  44.2 us (6%)
  other arithmetic  22.1 us (3%)
  between operations  14.3 us (2%)
    all_to_all x2, blocking collectives, shards(): lax.all_to_all(returned.reshape(owners, capacity, bands, patches), 'pairs...  378 us
    psum x2, waiting for transfers between devices, shards(): gathered = lax.psum(row_sum + incoming, 'rep')  97.3 us
    all_to_all x2, waiting for transfers between devices, shards(): lax.all_to_all(served_weights, 'pairs', split_axis=0, concat_axis=0, tile...  64.3 us
    all_to_all x1, waiting for transfers between devices, shards(): lax.all_to_all(served, 'pairs', split_axis=0, concat_axis=0, tiled=True)  38.4 us
    dot_general x10, matrix products, both_visit(): jnp.einsum('gij,gbi->gbj', kernel, jnp.take(weighted, row_ids, axis=0), p...  35.2 us
    dot_general x10, matrix products, both_visit(): jnp.einsum('gij,gbj->gbi', kernel, jnp.take(col_weights, safe, axis=0), p...  35 us
    all_to_all x2, starting transfers between devices, shards(): lax.all_to_all(served_weights, 'pairs', split_axis=0, concat_axis=0, tile...  23.3 us
    all_to_all x1, starting transfers between devices, shards(): lax.all_to_all(col_local, 'pairs', split_axis=0, concat_axis=0, tiled=True)  19.5 us
  transfers between devices with their start and end apart: 6, of which 6 were waited for; matrix products, arithmetic and copies ran while one was open for 1% of the time, Pallas kernels for 0%

commit v1 on v0

--- a/solution.py
+++ b/solution.py
@@ -148,7 +148,7 @@
             landed.reshape(slots, bands, patches),
             precision=lax.Precision.HIGHEST,
         )
-        gathered = lax.psum(row_sum + incoming, "rep")
+        gathered = jnp.sum(lax.all_gather(row_sum + incoming, "rep"), axis=0)
         radiosity = emission + reflect * gathered
     return radiosity
 

time: 800 us -> 703 us (0.88)
  waiting for transfers between devices: 212 us -> 115 us
  blocking collectives: 378 us -> 405 us
  between operations: 14.3 us -> 0.94 us
  starting transfers between devices: 50.3 us -> 40.4 us
    psum x2 -> x0, waiting for transfers between devices: 97.3 us -> none  [shards(): gathered = lax.psum(row_sum + incoming, 'rep')]
    all_gather x0 -> x2, blocking collectives: none -> 27.3 us  [shards(): gathered = jnp.sum(lax.all_gather(row_sum + incoming, 'rep'), axis=0)]
    all_to_all x2, starting transfers between devices: 23.3 us -> 13.5 us  [shards(): lax.all_to_all(served_weights, 'pairs', split_axis=0, concat_axis=0, tile...]
  transfers between devices with their start and end apart: 6 -> 4, of which waited for: 6 -> 4; matrix products, arithmetic and copies ran while one was open for 1% -> 1% of each run, Pallas kernels for 0% -> 0%
where the time goes in v1:
time: 703 us
  blocking collectives  405 us (58%)
  waiting for transfers between devices  115 us (16%)
  matrix products  74.8 us (11%)
  local copies, waits for them, and re-layouts  44.2 us (6%)
  starting transfers between devices  40.4 us (6%)
  other arithmetic  20.3 us (3%)
    all_to_all x2, blocking collectives, shards(): lax.all_to_all(returned.reshape(owners, capacity, bands, patches), 'pairs...  378 us
    all_to_all x2, waiting for transfers between devices, shards(): lax.all_to_all(served_weights, 'pairs', split_axis=0, concat_axis=0, tile...  64.4 us
    all_to_all x1, waiting for transfers between devices, shards(): lax.all_to_all(served, 'pairs', split_axis=0, concat_axis=0, tiled=True)  38.5 us
    dot_general x10, matrix products, both_visit(): jnp.einsum('gij,gbi->gbj', kernel, jnp.take(weighted, row_ids, axis=0), p...  35 us
    dot_general x10, matrix products, both_visit(): jnp.einsum('gij,gbj->gbi', kernel, jnp.take(col_weights, safe, axis=0), p...  34.9 us
    all_gather x2, blocking collectives, shards(): gathered = jnp.sum(lax.all_gather(row_sum + incoming, 'rep'), axis=0)  27.3 us
    all_to_all x1, starting transfers between devices, shards(): lax.all_to_all(col_local, 'pairs', split_axis=0, concat_axis=0, tiled=True)  19.5 us
  transfers between devices with their start and end apart: 4, of which 4 were waited for; matrix products, arithmetic and copies ran while one was open for 1% of the time, Pallas kernels for 0%

profile of v1, /device:TPU:2, one launch (start us, length us, event | category | flops | bytes accessed | tf_op | source)
XLA Modules:
  0.0 702.5 jit_solution(17231585219399181316)
XLA Ops:
  3.9 19.5 %all-to-all-start = ((s32[128,1,1]{2,1,0:T(1,128)}), s32[128,1,1]{2,1,0:T(1,128)S(1)}, u32[]{:S(2)}, u32[]{:S(2)}) async-start(s32[128,1,1]{2,1,0:T(1,128)} %get-tuple-element.311), calls=%async_computation | async-start | bytes 131072 | tf_op jit(solution)/shard_map/all_to_all | solution.py:95
  25.3 12.5 %all-to-all-done = s32[128,1,1]{2,1,0:T(1,128)S(1)} async-done(((s32[128,1,1]{2,1,0:T(1,128)}), s32[128,1,1]{2,1,0:T(1,128)S(1)}, u32[]{:S(2)}, u32[]{:S(2)}) %all-to-all-start) | async-done | bytes 544 | tf_op jit(solution)/shard_map/all_to_all | solution.py:95
  45.3 7.4 %all-to-all-start.2 = ((f32[128,1,6,256]{3,1,2,0:T(1,128)}), f32[128,1,6,256]{3,1,2,0:T(1,128)S(1)}, u32[]{:S(2)}, u32[]{:S(2)}) async-start(f32[128,1,6,256]{3,1,2,0:T(1,128)} %copy.105), calls=%async_computation.2 | async-start | bytes 1572864 | tf_op jit(solution)/shard_map/all_to_all | solution.py:97
  52.8 4.6 fusion.86
  59.1 38.5 %all-to-all-done.2 = f32[128,1,6,256]{3,1,2,0:T(1,128)S(1)} async-done(((f32[128,1,6,256]{3,1,2,0:T(1,128)}), f32[128,1,6,256]{3,1,2,0:T(1,128)S(1)}, u32[]{:S(2)}, u32[]{:S(2)}) %all-to-all-start.2) | async-done | bytes 786464 | tf_op jit(solution)/shard_map/all_to_all | solution.py:97
  97.6 6.7 all-to-all-start.1
  107.1 30.8 %all-to-all-done.1 = bf16[128,1,8,256]{3,2,1,0:T(8,128)(2,1)S(1)} async-done(((bf16[128,1,8,256]{3,2,1,0:T(8,128)(2,1)}), bf16[128,1,8,256]{3,2,1,0:T(8,128)(2,1)S(1)}, u32[]{:S(2)}, u32[]{:S(2)}) %all-to-all-start.1) | async-done | bytes 524320 | tf_op jit(solution)/shard_map/all_to_all | solution.py:110
  138.0 57.5 %while.24 = (s32[]{:T(128)}, f32[16,8,256]{2,0,1:T(8,128)S(1)}, f32[128,8,256]{2,1,0:T(8,128)S(1)}, s32[]{:T(128)}, s32[136]{0:T(256)S(1)}, /*index=5*/s32[128]{...) while((s32[]{:T(128)}, f32[16,8,256]{2,0,1:T(8,128)S(1)}, ...), condition=%wide.region_5.12_spmd, body=%wide.region_3.11_spmd.sunk | while | flops 48327124 | bytes 1844099 | solution.py:65
  140.8 3.5 fusion.122
  145.6 3.5 fusion.121
  152.3 3.5 fusion.122
  157.1 3.5 fusion.121
  163.8 3.5 fusion.122
  175.4 3.5 fusion.122
  186.9 3.5 fusion.122
  195.5 188.7 %all_to_all.31 = f32[128,1,8,256]{3,2,1,0:T(8,128)S(1)} all-to-all(f32[128,1,8,256]{3,2,1,0:T(8,128)S(1)} %bitcast.136), channel_id=1, replica_groups=mesh['pairs'=128,'rep'=4] {'pairs'}, dimensions={0} | all-to-all | bytes 2097152 | tf_op jit(solution)/shard_map/all_to_all | solution.py:138
  385.0 14.0 %all-gather = f32[64,8,256]{2,0,1:T(8,128)S(1)} all-gather(f32[16,8,256]{2,0,1:T(8,128)S(1)} %convolution_add_fusion.3), channel_id=2, replica_groups=mesh['pairs'=128,'rep'=4] {'rep'}, dimensions={0}, use_global_device_ids=true | all-gather | bytes 655360 | tf_op jit(solution)/shard_map/all_gather | solution.py:151
  400.8 6.8 all-to-all-start.4
  407.6 33.6 %all-to-all-done.4 = bf16[128,1,8,256]{3,2,1,0:T(8,128)(2,1)S(1)} async-done(((bf16[128,1,8,256]{3,2,1,0:T(8,128)(2,1)}), bf16[128,1,8,256]{3,2,1,0:T(8,128)(2,1)S(1)}, u32[]{:S(2)}, u32[]{:S(2)}) %all-to-all-start.4) | async-done | bytes 524320 | tf_op jit(solution)/shard_map/all_to_all | solution.py:110
  441.3 57.6 %while.25 = (s32[]{:T(128)}, f32[16,8,256]{2,0,1:T(8,128)S(1)}, f32[128,8,256]{2,1,0:T(8,128)S(1)}, s32[]{:T(128)}, s32[136]{0:T(256)S(1)}, /*index=5*/s32[128]{...) while((s32[]{:T(128)}, f32[16,8,256]{2,0,1:T(8,128)S(1)}, ...), condition=%wide.region_9.16_spmd, body=%wide.region_7.15_spmd.sunk | while | flops 48327124 | bytes 1844099 | solution.py:65
  444.1 3.5 fusion.132
  448.9 3.5 fusion.131
  455.7 3.5 fusion.132
  460.4 3.5 fusion.131
  467.2 3.5 fusion.132
  472.0 3.5 fusion.131
  478.7 3.5 fusion.132
  483.5 3.5 fusion.131
  490.2 3.5 fusion.132
  495.0 3.5 fusion.131
  498.8 188.8 %all_to_all.32 = f32[128,1,8,256]{3,2,1,0:T(8,128)S(1)} all-to-all(f32[128,1,8,256]{3,2,1,0:T(8,128)S(1)} %bitcast.137), channel_id=1, replica_groups=mesh['pairs'=128,'rep'=4] {'pairs'}, dimensions={0} | all-to-all | bytes 2097152 | tf_op jit(solution)/shard_map/all_to_all | solution.py:138
  688.3 13.3 %all-gather.1 = f32[64,8,256]{2,0,1:T(8,128)S(1)} all-gather(f32[16,8,256]{2,0,1:T(8,128)S(1)} %convolution_add_fusion.2), channel_id=3, replica_groups=mesh['pairs'=128,'rep'=4] {'rep'}, dimensions={0}, use_global_device_ids=true | all-gather | bytes 655360 | tf_op jit(solution)/shard_map/all_gather | solution.py:151
  (279 shorter events, 75.2 us)
Async XLA Ops:
  3.9 33.9 %all-to-all-start = ((s32[128,1,1]{2,1,0:T(1,128)}), s32[128,1,1]{2,1,0:T(1,128)S(1)}, u32[]{:S(2)}, u32[]{:S(2)}) async-start(s32[128,1,1]{2,1,0:T(1,128)} %get-tuple-element.311), calls=%async_computation | async-start | bytes 131072 | tf_op jit(solution)/shard_map/all_to_all | solution.py:95
  45.3 7.4 %copy-start = (f32[16,8,256]{2,1,0:T(8,128)S(1)}, f32[16,8,256]{2,1,0:T(8,128)}, u32[]{:S(2)}) copy-start(f32[16,8,256]{2,1,0:T(8,128)} %param.25) | copy-start | bytes 393220
  45.3 7.4 %copy-start.2 = (f32[16,256]{1,0:T(8,128)S(1)}, f32[16,256]{1,0:T(8,128)}, u32[]{:S(2)}) copy-start(f32[16,256]{1,0:T(8,128)} %param.24) | copy-start | bytes 49156
  45.3 52.3 %all-to-all-start.2 = ((f32[128,1,6,256]{3,1,2,0:T(1,128)}), f32[128,1,6,256]{3,1,2,0:T(1,128)S(1)}, u32[]{:S(2)}, u32[]{:S(2)}) async-start(f32[128,1,6,256]{3,1,2,0:T(1,128)} %copy.105), calls=%async_computation.2 | async-start | bytes 1572864 | tf_op jit(solution)/shard_map/all_to_all | solution.py:97
  97.6 40.3 %all-to-all-start.1 = ((bf16[128,1,8,256]{3,2,1,0:T(8,128)(2,1)}), bf16[128,1,8,256]{3,2,1,0:T(8,128)(2,1)S(1)}, u32[]{:S(2)}, u32[]{:S(2)}) async-start(bf16[128,1,8,256]{3,2,1,0:T(8,128)(2,1)} %fusion.67), calls=%async_computation.1 | async-start | bytes 1048576 | tf_op jit(solution)/shard_map/all_to_all | solution.py:110
  384.2 14.8 %copy-start.1 = (f32[16,8,256]{2,1,0:T(8,128)S(1)}, f32[16,8,256]{2,1,0:T(8,128)}, u32[]{:S(2)}) copy-start(f32[16,8,256]{2,1,0:T(8,128)} %param.26) | copy-start | bytes 393220
  400.8 40.4 %all-to-all-start.4 = ((bf16[128,1,8,256]{3,2,1,0:T(8,128)(2,1)}), bf16[128,1,8,256]{3,2,1,0:T(8,128)(2,1)S(1)}, u32[]{:S(2)}, u32[]{:S(2)}) async-start(bf16[128,1,8,256]{3,2,1,0:T(8,128)(2,1)} %fusion.66), calls=%async_computation.4 | async-start | bytes 1048576 | tf_op jit(solution)/shard_map/all_to_all | solution.py:110
